TPU v7x, 128 devices: a whole 4x4x4 slice. The times are simulated.
128 devices in a mesh: phi: 16 (over y_hi, z, core), gz: 8 (over y_lo, x).
Axes of the slice: x: 4, y: 4 (y_hi: 2, y_lo: 2; y = y_hi * 2 + y_lo), z: 4, core: 2. Of those that a mesh axis runs over, the one named last changes fastest.
Arguments:
- electric_radial: float32 [192, 128, 2048], P('gz', None, 'phi'), may hold values from -6 to 6
- electric_azimuth: float32 [192, 128, 2048], P('gz', None, 'phi'), may hold values from -6 to 6
- electric_height: float32 [192, 128, 2048], P('gz', None, 'phi'), may hold values from -6 to 6
- magnetic_radial: float32 [192, 128, 2048], P('gz', None, 'phi'), may hold values from -6 to 6
- magnetic_azimuth: float32 [192, 128, 2048], P('gz', None, 'phi'), may hold values from -6 to 6
- magnetic_height: float32 [192, 128, 2048], P('gz', None, 'phi'), may hold values from -6 to 6
- material: int32 [192, 128, 2048], P('gz', None, 'phi'), may hold values from 0 to 7
- permittivity: float32 [8], replicated, may hold values from 1 to 10
- conductivity: float32 [8], replicated, may hold values from 0.05 to 5
- mode_cutoff: int32 [32], replicated, may hold values from 1 to 127, as said below
Outputs:
- updated_electric_radial: float32 [192, 128, 2048], P('gz', None, 'phi')
- updated_electric_azimuth: float32 [192, 128, 2048], P('gz', None, 'phi')
- updated_electric_height: float32 [192, 128, 2048], P('gz', None, 'phi')
- updated_magnetic_radial: float32 [192, 128, 2048], P('gz', None, 'phi')
- updated_magnetic_azimuth: float32 [192, 128, 2048], P('gz', None, 'phi')
- updated_magnetic_height: float32 [192, 128, 2048], P('gz', None, 'phi')
Inputs may be any that keep to these rules, and one draw needn't show every extreme that they name: `mode_cutoff`: cutoffs never fall from one filtered row to the next outward, and the outermost filtered row's cutoff is 127.
All inputs are finite; a program needn't handle non-finite values.
Results may differ from a plain program's by a relative error of at most 0.00005.
Values sent between devices are 32-bit elements; how exact they have to be, the bound alone decides.
A program may use at most 128 MiB of HBM per device.

v0:
```python
import math
import jax
import jax.numpy as jnp
from jax import lax
from jax.sharding import PartitionSpec as P

KMAX = 128
NF = 32
NMAT = 8
inner_radius = 64.0
time_step = 0.2


def shifted(block, axis, distance):
    devices = range(lax.axis_size(axis))
    route = [((i - distance) % len(devices), i) for i in devices]
    return lax.ppermute(block, axis, route)


def shifted_2(block, axis, distance):
    devices = range(lax.axis_size(axis))
    route = [(i - distance, i) for i in devices if i - distance in devices]
    return lax.ppermute(block, axis, route)


def radial_forward(values):
    zero_slab = jnp.zeros_like(values[:, :1, :])
    return jnp.concatenate([values[:, 1:, :], zero_slab], axis=1) - values


def radial_backward(values):
    zero_slab = jnp.zeros_like(values[:, :1, :])
    return values - jnp.concatenate([zero_slab, values[:, :-1, :]], axis=1)


def ahead_azimuth(values, border):
    return jnp.concatenate([values[:, :, 1:], border[:, :, None]], axis=2) - values


def behind_azimuth(values, border):
    return values - jnp.concatenate([border[:, :, None], values[:, :, :-1]], axis=2)


def ahead_height(values, border):
    return jnp.concatenate([values[1:], border[None]], axis=0) - values


def behind_height(values, border):
    return values - jnp.concatenate([border[None], values[:-1]], axis=0)


def cycle_basis(offset, length, cycle_size):
    columns = offset + jnp.arange(length, dtype=jnp.int32)
    mode_index = jnp.arange(KMAX, dtype=jnp.int32)
    angles = (columns[:, None] * mode_index[None, :] % cycle_size).astype(jnp.float32) * (
        2.0 * math.pi / cycle_size
    )
    return jnp.concatenate([jnp.cos(angles), jnp.sin(angles)], axis=1)


def mode_weights(cutoffs, cycle_size):
    mode_index = jnp.arange(KMAX, dtype=jnp.int32)
    scaled = jnp.where(mode_index == 0, 1.0, 2.0).astype(jnp.float32) / cycle_size
    weights = jnp.where(mode_index[None, :] <= cutoffs[:, None], scaled[None, :], 0.0)
    return jnp.concatenate([weights, weights], axis=1)


def transform(block, basis):
    flat = block.reshape(-1, block.shape[-1])
    result = jnp.dot(
        flat, basis, precision=lax.Precision.HIGHEST, preferred_element_type=jnp.float32
    )
    return result.reshape(block.shape[:-1] + (basis.shape[1],))


def synthesize(spectrum, basis):
    flat = spectrum.reshape(-1, spectrum.shape[-1])
    result = jnp.dot(
        flat, basis.T, precision=lax.Precision.HIGHEST, preferred_element_type=jnp.float32
    )
    return result.reshape(spectrum.shape[:-1] + (basis.shape[0],))


def cycle_filter(stacked, mode_cutoff):
    cycle_count = lax.axis_size("phi")
    local_width = stacked.shape[3]
    cycle_size = cycle_count * local_width
    offset = lax.axis_index("phi") * local_width
    weights = mode_weights(mode_cutoff, cycle_size)
    local_basis = cycle_basis(offset, local_width, cycle_size)
    portion = lax.all_gather(stacked, "phi", axis=3, tiled=True)
    spectrum = transform(portion, cycle_basis(jnp.int32(0), portion.shape[3], cycle_size))
    return synthesize(spectrum * weights[None, None], local_basis)


def filter_three(first, second, third, mode_cutoff):
    stacked = jnp.stack([first[:, :NF], second[:, :NF], third[:, :NF]])
    filtered = cycle_filter(stacked, mode_cutoff)
    return (
        jnp.concatenate([filtered[0], first[:, NF:]], axis=1),
        jnp.concatenate([filtered[1], second[:, NF:]], axis=1),
        jnp.concatenate([filtered[2], third[:, NF:]], axis=1),
    )


def local(
    electric_radial,
    electric_azimuth,
    electric_height,
    magnetic_radial,
    magnetic_azimuth,
    magnetic_height,
    material,
    permittivity,
    conductivity,
    mode_cutoff,
):
    local_width = electric_radial.shape[2]
    radial_rows = electric_radial.shape[1]
    node_radius = (inner_radius + jnp.arange(radial_rows, dtype=jnp.float32))[None, :, None]
    center_radius = node_radius + 0.5
    angle_step = 2.0 * math.pi / (lax.axis_size("phi") * local_width)
    border_height, border_radial = shifted(
        (electric_height[:, :, 0], electric_radial[:, :, 0]), "phi", -1
    )
    upper_azimuth, upper_radial = shifted_2((electric_azimuth[0], electric_radial[0]), "gz", -1)
    radial_half = magnetic_radial - time_step * (
        ahead_azimuth(electric_height, border_height) / (node_radius * angle_step)
        - ahead_height(electric_azimuth, upper_azimuth)
    )
    azimuth_half = magnetic_azimuth - time_step * (
        ahead_height(electric_radial, upper_radial) - radial_forward(electric_height)
    )
    height_half = magnetic_height - time_step * (
        radial_forward(node_radius * electric_azimuth) / center_radius
        - ahead_azimuth(electric_radial, border_radial) / (center_radius * angle_step)
    )
    new_hr, new_hp, new_hz = filter_three(radial_half, azimuth_half, height_half, mode_cutoff)
    epsilon = jnp.zeros(material.shape, jnp.float32)
    sigma_cell = jnp.zeros(material.shape, jnp.float32)
    for number in range(NMAT):
        epsilon = jnp.where(material == number, permittivity[number], epsilon)
        sigma_cell = jnp.where(material == number, conductivity[number], sigma_cell)
    losses = sigma_cell * time_step / (2.0 * epsilon)
    keep_factor = (1.0 - losses) / (1.0 + losses)
    drive_factor = time_step / (epsilon * (1.0 + losses))
    before_height, before_radial = shifted((new_hz[:, :, -1], new_hr[:, :, -1]), "phi", 1)
    lower_azimuth, lower_radial = shifted_2((new_hp[-1], new_hr[-1]), "gz", 1)
    radial_next = keep_factor * electric_radial + drive_factor * (
        behind_azimuth(new_hz, before_height) / (center_radius * angle_step)
        - behind_height(new_hp, lower_azimuth)
    )
    azimuth_next = keep_factor * electric_azimuth + drive_factor * (
        behind_height(new_hr, lower_radial) - radial_backward(new_hp)
    )
    height_next = keep_factor * electric_height + drive_factor * (
        radial_backward(center_radius * new_hp) / node_radius
        - behind_azimuth(new_hr, before_radial) / (node_radius * angle_step)
    )
    new_er, new_ep, new_ez = filter_three(radial_next, azimuth_next, height_next, mode_cutoff)
    return (new_er, new_ep, new_ez, new_hr, new_hp, new_hz)


def solution(mesh):
    placed = (
        P("gz", None, "phi"),
        P("gz", None, "phi"),
        P("gz", None, "phi"),
        P("gz", None, "phi"),
        P("gz", None, "phi"),
        P("gz", None, "phi"),
        P("gz", None, "phi"),
        P(),
        P(),
        P(),
    )
    return jax.shard_map(
        local,
        mesh=mesh,
        in_specs=placed,
        out_specs=(
            P("gz", None, "phi"),
            P("gz", None, "phi"),
            P("gz", None, "phi"),
            P("gz", None, "phi"),
            P("gz", None, "phi"),
            P("gz", None, "phi"),
        ),
        check_vma=False,
    )
```

profile of v0, /device:TPU:1, one launch (start us, length us, event | category | flops | bytes accessed | tf_op | source)
XLA Modules:
  0.0 429.9 jit_solution(6858078280458074750)
XLA Ops:
  7.2 2.0 copy.33
  9.3 1.5 collective-permute-start
  10.7 0.5 copy.34
  11.2 6.2 %collective-permute-start.3 = (f32[24,128]{1,0:T(8,128)S(1)}, f32[24,128]{1,0:T(8,128)S(1)}, u32[]{:S(2)}, u32[]{:S(2)}) collective-permute-start(f32[24,128]{1,0:T(8,128)S(1)} %bitcast.96), channel_id=1, source_target_pairs={{8,0},{16,8},{24,16},{32,24},{40,32},{48,40},{56,48},{64,56},{72,6... | collective-permute-start | bytes 36872 | tf_op jit(solution)/shard_map/ppermute | solution.py:17
  17.4 1.3 collective-permute-start.2
  18.7 1.3 collective-permute-start.1
  20.1 1.2 slice.186
  21.3 1.3 slice.189
  22.6 0.6 copy-done.1
  23.3 1.6 slice.184
  24.9 1.3 slice.191
  26.2 1.6 slice.194
  27.8 1.7 copy.29
  29.5 1.7 copy.27
  31.2 5.6 %fusion.14 = (f32[24,128,128]{2,1,0:T(8,128)S(1)}, f32[24,128,128]{2,1,0:T(8,128)S(1)}, f32[24,128,128]{2,1,0:T(8,128)S(1)}) fusion(f32[24,128,128]{2,1,0:T(8,128)} %param.13, f32[24,128,128]{2,1,0:T(8,128)S(1)} %copy-done.1, f32[24,128,1]{2,1,0:T(8,128)} %copy.27, f32[24,128,127]{2,1,0:T(8,128)} %slice.184, f32[24,128,128]{2,1,0:T(8,128)} %param.11, ...), kind=kLoop, calls=%fused_computation.37 | loop fusion | flops 5898240 | bytes 18863104 | tf_op jit(solution)/shard_map/sub | solution.py:127
  37.0 2.3 copy-done.20
  39.4 0.5 copy-done.21
  39.8 1.0 fusion.21
  40.9 1.0 copy-done.16
  41.9 1.1 pad_maximum_fusion.6
  43.3 0.7 fusion.66
  44.0 0.7 fusion.65
  45.1 5.0 %fusion.41 = (f32[2048,128]{1,0:T(8,128)}, f32[2048,128]{1,0:T(8,128)}) fusion(), kind=kLoop, calls=%fused_computation.93 | loop fusion | flops 3670016 | bytes 2097152 | tf_op jit(solution)/shard_map/sin | solution.py:58
  50.1 1.5 slice.240
  51.9 1.1 slice.233
  53.0 0.8 copy-done.17
  53.8 1.2 slice.227
  55.0 118.5 %all-gather.3.cloned.1.call-done = f32[3,24,32,2048]{3,2,1,0:T(8,128)} async-done(((f32[3,24,32,128]{3,2,1,0:T(8,128)}), f32[3,24,32,2048]{3,2,1,0:T(8,128)}) %all-gather.3.cloned.1.call-update) | async-done | bytes 18874384 | tf_op jit(solution)/shard_map/all_gather | solution.py:91
  173.5 18.5 %fusion.2 = f32[3,24,32,256]{3,2,1,0:T(8,128)S(1)} fusion(f32[3,24,32,2048]{3,2,1,0:T(8,128)} %all-gather.3.cloned.1.call-done, f32[2048,128]{1,0:T(8,128)} %get-tuple-element.50, f32[2048,128]{1,0:T(8,128)} %get-tuple-element.51, f32[32,256]{1,0:T(8,128)S(1)} %pad_maximum_fusion.11), kind=kOutput, calls=%fused_computation.24 | convolution fusion | flops 14496628736 | bytes 23363584 | tf_op jit(solution)/shard_map/dot_general | solution.py:70
  192.0 2.0 fusion.44
  194.1 0.9 fusion.9
  195.0 0.6 fusion.53
  195.7 1.2 fusion.34
  196.9 0.6 copy-done.3
  197.5 1.2 fusion.33
  198.7 1.3 fusion.7
  200.0 1.3 fusion.10
  201.3 0.5 copy-done.5
  201.8 0.9 fusion.5
  202.7 1.3 fusion.6
  204.0 3.7 collective-permute-start.6
  207.7 0.6 fusion.54
  208.3 3.1 collective-permute-start.5
  211.4 0.6 copy-done.38
  212.0 2.4 copy.31
  214.4 2.4 copy.30
  216.8 15.9 %fusion.28 = (f32[24,128,128]{2,1,0:T(8,128)S(1)}, f32[24,128,128]{2,1,0:T(8,128)S(1)}, pred[24,128,128]{2,1,0:T(8,128)(4,1)S(1)}, pred[24,128,128]{2,1,0:T(8,12...) fusion(f32[23,128,128]{2,1,0:T(8,128)} %fusion.34, ...), kind=kLoop, calls=%fused_computation.57 | loop fusion | flops 16121856 | bytes 17289280 | tf_op jit(solution)/shard_map/add | solution.py:153
  233.0 0.8 copy-done.24
  233.9 1.0 copy-done.6
  234.9 1.3 copy-done.13
  236.3 14.9 %fusion.25 = (f32[24,128,128]{2,1,0:T(8,128)S(1)}, f32[24,128,128]{2,1,0:T(8,128)}) fusion(f32[24,128,127]{2,1,0:T(8,128)S(1)} %copy-done.13, f32[24,128,1]{2,1,0:T(8,128)S(1)} %copy-done.14, f32[24,128,128]{2,1,0:T(8,128)S(1)} %get-tuple-element.16, f32[23,128,128]{2,1,0:T(8,128)S(1)} %copy-done.26, f32[1,128,128]{2,1,0:T(8,128)} %bitcast.34, ...), kind=kLoop, calls=%fused_computation.52 | loop fusion | flops 13369344 | bytes 14156352 | tf_op jit(solution)/shard_map/add | solution.py:149
  251.3 13.2 %fusion.32 = f32[24,128,128]{2,1,0:T(8,128)S(1)} fusion(f32[24,128,128]{2,1,0:T(8,128)S(1)} %get-tuple-element.7, f32[24,128,127]{2,1,0:T(8,128)S(1)} %copy-done.15, f32[24,128,1]{2,1,0:T(8,128)S(1)} %copy-done.18, f32[24,127,128]{2,1,0:T(8,128)S(1)} %bitcast.87, f32[24,128,128]{2,1,0:T(8,128)S(1)} %copy-done.2, f32[128]{0:T(128)S(1)} %copy-done.42, ...), kind=kLoop, calls=%fused_computation.62 | loop fusion | flops 13369344 | bytes 12572224 | tf_op jit(solution)/shard_map/add | solution.py:156
  264.5 1.2 pad_maximum_fusion.7
  266.0 2.4 slice.257
  268.5 1.1 slice.255
  269.6 127.1 %all-gather.5.cloned.1.call-done = f32[3,24,32,2048]{3,2,1,0:T(8,128)} async-done(((f32[3,24,32,128]{3,2,1,0:T(8,128)}), f32[3,24,32,2048]{3,2,1,0:T(8,128)}) %all-gather.5.cloned.1.call-update) | async-done | bytes 18874384 | tf_op jit(solution)/shard_map/all_gather | solution.py:91
  396.7 18.2 %fusion.3 = f32[3,24,32,256]{3,2,1,0:T(8,128)S(1)} fusion(f32[3,24,32,2048]{3,2,1,0:T(8,128)} %all-gather.5.cloned.1.call-done, f32[2048,128]{1,0:T(8,128)S(1)} %copy-done.8, f32[2048,128]{1,0:T(8,128)S(1)} %copy-done.9, f32[32,256]{1,0:T(8,128)S(1)} %copy-done.30), kind=kOutput, calls=%fused_computation.25 | convolution fusion | flops 14496628736 | bytes 23363584 | tf_op jit(solution)/shard_map/dot_general | solution.py:70
  414.9 2.0 fusion.43
  417.0 1.2 slice-done
  418.2 1.3 pad_maximum_fusion.5
  419.5 0.5 copy-done.28
  420.0 1.3 pad_maximum_fusion.4
  421.3 0.5 copy-done.27
  421.8 1.3 pad_maximum_fusion.3
  (113 shorter events, 2.3 us)
Async XLA Ops:
  7.2 3.6 copy-start
  7.2 166.3 %all-gather.3.cloned.1.call-start = ((), (), s32[]{:S(2)}) async-start(), calls=%async_computation | async-start | bytes 20054016 | tf_op jit(solution)/shard_map/all_gather | solution.py:91
  7.2 11.5 %copy-start.7 = (f32[24,128,128]{2,1,0:T(8,128)S(1)}, f32[24,128,128]{2,1,0:T(8,128)}, u32[]{:S(2)}) copy-start(f32[24,128,128]{2,1,0:T(8,128)} %param.11) | copy-start | bytes 4718596
  9.3 20.2 %collective-permute-start = (f32[24,128]{1,0:T(8,128)S(1)}, f32[24,128]{1,0:T(8,128)S(1)}, u32[]{:S(2)}, u32[]{:S(2)}) collective-permute-start(f32[24,128]{1,0:T(8,128)S(1)} %bitcast.94), channel_id=1, source_target_pairs={{8,0},{16,8},{24,16},{32,24},{40,32},{48,40},{56,48},{64,56},{72,6... | collective-permute-start | bytes 36872 | tf_op jit(solution)/shard_map/ppermute | solution.py:17
  11.2 16.6 %collective-permute-start.3 = (f32[24,128]{1,0:T(8,128)S(1)}, f32[24,128]{1,0:T(8,128)S(1)}, u32[]{:S(2)}, u32[]{:S(2)}) collective-permute-start(f32[24,128]{1,0:T(8,128)S(1)} %bitcast.96), channel_id=1, source_target_pairs={{8,0},{16,8},{24,16},{32,24},{40,32},{48,40},{56,48},{64,56},{72,6... | collective-permute-start | bytes 36872 | tf_op jit(solution)/shard_map/ppermute | solution.py:17
  17.4 13.7 %collective-permute-start.2 = (f32[128,128]{1,0:T(8,128)S(1)}, f32[128,128]{1,0:T(8,128)S(1)}, u32[]{:S(2)}, u32[]{:S(2)}) collective-permute-start(f32[128,128]{1,0:T(8,128)S(1)} %slice_bitcast_fusion.6), channel_id=1, source_target_pairs={{1,0},{2,1},{3,2},{4,3},{5,4},{6,5},{7,6},{9,8},{10,9},{11,10},{12... | collective-permute-start | bytes 196616 | tf_op jit(solution)/shard_map/ppermute | solution.py:23
  18.7 12.4 %collective-permute-start.1 = (f32[128,128]{1,0:T(8,128)S(1)}, f32[128,128]{1,0:T(8,128)S(1)}, u32[]{:S(2)}, u32[]{:S(2)}) collective-permute-start(f32[128,128]{1,0:T(8,128)S(1)} %slice_bitcast_fusion.7), channel_id=1, source_target_pairs={{1,0},{2,1},{3,2},{4,3},{5,4},{6,5},{7,6},{9,8},{10,9},{11,10},{12... | collective-permute-start | bytes 196616 | tf_op jit(solution)/shard_map/ppermute | solution.py:23
  20.0 11.1 %copy-start.39 = (f32[128]{0:T(128)}, f32[128]{0:T(128)S(1)}, u32[]{:S(2)}) copy-start(f32[128]{0:T(128)S(1)} %broadcast_multiply_fusion.3) | copy-start | bytes 1540
  20.1 16.9 %copy-start.43 = (f32[128]{0:T(128)}, f32[128]{0:T(128)S(1)}, u32[]{:S(2)}) copy-start(f32[128]{0:T(128)S(1)} %get-tuple-element.49) | copy-start | bytes 1540
  20.1 11.1 %copy-start.41 = (f32[128]{0:T(128)}, f32[128]{0:T(128)S(1)}, u32[]{:S(2)}) copy-start(f32[128]{0:T(128)S(1)} %iota_add_fusion.2) | copy-start | bytes 1540
  21.3 2.0 copy-start.1
  31.2 5.9 %copy-start.31 = (f32[24,128,128]{2,1,0:T(8,128)S(1)}, f32[24,128,128]{2,1,0:T(8,128)}, u32[]{:S(2)}) copy-start(f32[24,128,128]{2,1,0:T(8,128)} %param.15) | copy-start | bytes 4718596
  36.8 4.0 copy-start.10
  36.8 4.0 copy-start.12
  36.8 2.5 copy-start.20
  36.8 3.0 copy-start.21
  40.8 1.1 copy-start.16
  41.9 1.4 copy-start.36
  41.9 2.1 copy-start.37
  41.9 2.8 copy-start.45
  43.1 353.6 %all-gather.5.cloned.1.call-start = ((), (), s32[]{:S(2)}) async-start(), calls=%async_computation.1 | async-start | bytes 20054016 | tf_op jit(solution)/shard_map/all_gather | solution.py:91
  44.8 128.7 %copy-start.29 = (f32[32,256]{1,0:T(8,128)}, f32[32,256]{1,0:T(8,128)S(1)}, u32[]{:S(2)}) copy-start(f32[32,256]{1,0:T(8,128)S(1)} %pad_maximum_fusion.11) | copy-start | bytes 98308
  45.1 146.9 %copy-start.32 = (f32[128,128]{1,0:T(8,128)}, f32[128,128]{1,0:T(8,128)S(1)}, u32[]{:S(2)}) copy-start(f32[128,128]{1,0:T(8,128)S(1)} %get-tuple-element.44) | copy-start | bytes 196612
  45.1 146.9 %copy-start.34 = (f32[128,128]{1,0:T(8,128)}, f32[128,128]{1,0:T(8,128)S(1)}, u32[]{:S(2)}) copy-start(f32[128,128]{1,0:T(8,128)S(1)} %get-tuple-element.45) | copy-start | bytes 196612
  50.1 1.8 copy-start.11
  51.9 2.0 copy-start.17
  194.1 8.6 %copy-start.22 = (f32[768,128]{1,0:T(8,128)}, f32[768,128]{1,0:T(8,128)S(1)}, u32[]{:S(2)}) copy-start(f32[768,128]{1,0:T(8,128)S(1)} %get-tuple-element.27) | copy-start | bytes 1179652
  195.7 1.8 copy-start.3
  200.0 1.8 copy-start.5
  204.0 10.4 %collective-permute-start.4 = (f32[24,128]{1,0:T(8,128)S(1)}, f32[24,128]{1,0:T(8,128)}, u32[]{:S(2)}, u32[]{:S(2)}) collective-permute-start(f32[24,128]{1,0:T(8,128)S(1)} %fusion.5), channel_id=1, source_target_pairs={{120,0},{0,8},{8,16},{16,24},{24,32},{32,40},{40,48},{48,56},{56,6... | collective-permute-start | bytes 36872 | tf_op jit(solution)/shard_map/ppermute | solution.py:17
  204.0 7.4 %collective-permute-start.7 = (f32[24,128]{1,0:T(8,128)S(1)}, f32[24,128]{1,0:T(8,128)S(1)}, u32[]{:S(2)}, u32[]{:S(2)}) collective-permute-start(f32[24,128]{1,0:T(8,128)S(1)} %fusion.9), channel_id=1, source_target_pairs={{120,0},{0,8},{8,16},{16,24},{24,32},{32,40},{40,48},{48,56},{56,6... | collective-permute-start | bytes 36872 | tf_op jit(solution)/shard_map/ppermute | solution.py:17
  204.0 12.8 %collective-permute-start.6 = (f32[128,128]{1,0:T(8,128)}, f32[128,128]{1,0:T(8,128)}, u32[]{:S(2)}, u32[]{:S(2)}) collective-permute-start(f32[128,128]{1,0:T(8,128)} %fusion.53), channel_id=1, source_target_pairs={{0,1},{1,2},{2,3},{3,4},{4,5},{5,6},{6,7},{8,9},{9,10},{10,11},{11... | collective-permute-start | bytes 196616 | tf_op jit(solution)/shard_map/ppermute | solution.py:23
  208.3 25.6 %collective-permute-start.5 = (f32[128,128]{1,0:T(8,128)}, f32[128,128]{1,0:T(8,128)}, u32[]{:S(2)}, u32[]{:S(2)}) collective-permute-start(f32[128,128]{1,0:T(8,128)} %fusion.54), channel_id=1, source_target_pairs={{0,1},{1,2},{2,3},{3,4},{4,5},{5,6},{6,7},{8,9},{9,10},{10,11},{11... | collective-permute-start | bytes 196616 | tf_op jit(solution)/shard_map/ppermute | solution.py:23
  211.4 0.6 copy-start.38
  216.8 17.1 %copy-start.14 = (f32[24,128,1]{2,1,0:T(8,128)S(1)}, f32[24,128,1]{2,1,0:T(8,128)}, u32[]{:S(2)}) copy-start(f32[24,128,1]{2,1,0:T(8,128)} %copy.30) | copy-start | bytes 36868
  216.8 17.1 %copy-start.26 = (f32[23,128,128]{2,1,0:T(8,128)S(1)}, f32[23,128,128]{2,1,0:T(8,128)}, u32[]{:S(2)}) copy-start(f32[23,128,128]{2,1,0:T(8,128)} %fusion.33) | copy-start | bytes 4521988
  232.7 1.2 copy-start.24
  232.7 18.6 %copy-start.4 = (f32[24,128,128]{2,1,0:T(8,128)}, f32[24,128,128]{2,1,0:T(8,128)S(1)}, u32[]{:S(2)}) copy-start(f32[24,128,128]{2,1,0:T(8,128)S(1)} %get-tuple-element.16) | copy-start | bytes 4718596
  232.7 18.5 %copy-start.25 = (f32[24,128,128]{2,1,0:T(8,128)}, f32[24,128,128]{2,1,0:T(8,128)S(1)}, u32[]{:S(2)}) copy-start(f32[24,128,128]{2,1,0:T(8,128)S(1)} %get-tuple-element.7) | copy-start | bytes 4718596
  232.7 2.2 copy-start.6
  232.7 3.4 copy-start.13
  232.8 3.5 copy-start.23
  232.8 3.5 copy-start.44
  236.2 15.0 %copy-start.2 = (f32[24,128,128]{2,1,0:T(8,128)S(1)}, f32[24,128,128]{2,1,0:T(8,128)}, u32[]{:S(2)}) copy-start(f32[24,128,128]{2,1,0:T(8,128)} %param.12) | copy-start | bytes 4718596
  236.2 15.0 %copy-start.15 = (f32[24,128,127]{2,1,0:T(8,128)S(1)}, f32[24,128,127]{2,1,0:T(8,128)}, u32[]{:S(2)}) copy-start(f32[24,128,127]{2,1,0:T(8,128)} %fusion.10) | copy-start | bytes 4681732
  236.2 15.0 %copy-start.18 = (f32[24,128,1]{2,1,0:T(8,128)S(1)}, f32[24,128,1]{2,1,0:T(8,128)}, u32[]{:S(2)}) copy-start(f32[24,128,1]{2,1,0:T(8,128)} %copy.31) | copy-start | bytes 36868
  236.3 15.1 %copy-start.40 = (f32[128]{0:T(128)S(1)}, f32[128]{0:T(128)}, u32[]{:S(2)}) copy-start(f32[128]{0:T(128)} %copy-done.39) | copy-start | bytes 1540
  236.3 15.1 %copy-start.42 = (f32[128]{0:T(128)S(1)}, f32[128]{0:T(128)}, u32[]{:S(2)}) copy-start(f32[128]{0:T(128)} %copy-done.41) | copy-start | bytes 1540
  264.5 1.5 copy-start.19
  269.6 127.1 %copy-start.8 = (f32[2048,128]{1,0:T(8,128)S(1)}, f32[2048,128]{1,0:T(8,128)}, u32[]{:S(2)}) copy-start(f32[2048,128]{1,0:T(8,128)} %get-tuple-element.50) | copy-start | bytes 3145732
  269.6 127.1 %copy-start.9 = (f32[2048,128]{1,0:T(8,128)S(1)}, f32[2048,128]{1,0:T(8,128)}, u32[]{:S(2)}) copy-start(f32[2048,128]{1,0:T(8,128)} %get-tuple-element.51) | copy-start | bytes 3145732
  269.6 127.1 %copy-start.30 = (f32[32,256]{1,0:T(8,128)S(1)}, f32[32,256]{1,0:T(8,128)}, u32[]{:S(2)}) copy-start(f32[32,256]{1,0:T(8,128)} %copy-done.29) | copy-start | bytes 98308
  269.6 145.3 %copy-start.33 = (f32[128,128]{1,0:T(8,128)S(1)}, f32[128,128]{1,0:T(8,128)}, u32[]{:S(2)}) copy-start(f32[128,128]{1,0:T(8,128)} %copy-done.32) | copy-start | bytes 196612
  269.6 145.4 %copy-start.35 = (f32[128,128]{1,0:T(8,128)S(1)}, f32[128,128]{1,0:T(8,128)}, u32[]{:S(2)}) copy-start(f32[128,128]{1,0:T(8,128)} %copy-done.34) | copy-start | bytes 196612
  416.9 1.3 slice-start
  418.2 1.8 copy-start.28
  420.0 1.8 copy-start.27
Sparse Core Ops, SparseCore 0:
  43.2 130.2 all-gather.2
  266.2 130.4 all-gather.4
where the time goes:
time: 431 us; the launch traced here: 430 us
  waiting for transfers between devices  246 us (57%)
  other arithmetic  71.7 us (17%)
  matrix products  40.8 us (9%)
  local copies, waits for them, and re-layouts  39.9 us (9%)
  starting transfers between devices  17.3 us (4%)
  between operations  14.7 us (3%)
    all_gather x2, waiting for transfers between devices, cycle_filter(): portion = lax.all_gather(stacked, 'phi', axis=3, tiled=True)  246 us
    dot_general x2, matrix products, transform(): jnp.dot(flat, basis, precision=lax.Precision.HIGHEST, preferred_element_t...  36.8 us
    add x1, other arithmetic, local(): keep_factor * electric_azimuth  15.9 us
    add x1, other arithmetic, local(): keep_factor * electric_radial  14.9 us
    unnamed x94, local copies, waits for them, and re-layouts  14.4 us
    add x1, other arithmetic, local(): keep_factor * electric_height  13.2 us
    ppermute x4, starting transfers between devices, shifted_2(): return lax.ppermute(block, axis, route)  9.37 us
  transfers between devices with their start and end apart: 10, of which 2 were waited for; matrix products, arithmetic and copies ran while one was open for 11% of the time, Pallas kernels for 0%

commit v1 on v0

--- a/solution.py
+++ b/solution.py
@@ -88,7 +88,16 @@
     offset = lax.axis_index("phi") * local_width
     weights = mode_weights(mode_cutoff, cycle_size)
     local_basis = cycle_basis(offset, local_width, cycle_size)
-    portion = lax.all_gather(stacked, "phi", axis=3, tiled=True)
+    figure_create = lambda array_here, group_axis: jnp.concatenate(
+        jax.lax.all_to_all(
+            jnp.stack([array_here for _ in range(jax.lax.axis_size(group_axis))]),
+            group_axis,
+            split_axis=0,
+            concat_axis=0,
+        ),
+        axis=3,
+    )
+    portion = figure_create(stacked, "phi")
     spectrum = transform(portion, cycle_basis(jnp.int32(0), portion.shape[3], cycle_size))
     return synthesize(spectrum * weights[None, None], local_basis)
 

time: 431 us -> 832 us (1.93); the launches traced: 430 us -> 818 us
  waiting for transfers between devices: 246 us -> 548 us
  local copies, waits for them, and re-layouts: 39.9 us -> 103 us
  starting transfers between devices: 17.3 us -> 42 us
  between operations: 14.7 us -> 1.84 us
  other arithmetic: 71.7 us -> 82.8 us
    all_to_all x0 -> x2, waiting for transfers between devices: none -> 548 us  [cycle_filter(): jax.lax.all_to_all(jnp.stack([array_here for _ in range(jax.lax.axis_size...]
    all_gather x2 -> x0, waiting for transfers between devices: 246 us -> none  [cycle_filter(): portion = lax.all_gather(stacked, 'phi', axis=3, tiled=True)]
    unnamed x94 -> x133, local copies, waits for them, and re-layouts: 14.4 us -> 39.8 us
    another operation x0 -> x2, local copies, waits for them, and re-layouts: none -> 17.8 us  [cycle_filter(): jnp.stack([array_here for _ in range(jax.lax.axis_size(group_axis))])]
    another operation x5 -> x11, local copies, waits for them, and re-layouts: 0.17 us -> 17 us  [filter_three(): stacked = jnp.stack([first[:, :NF], second[:, :NF], third[:, :NF]])]
    all_to_all x0 -> x2, starting transfers between devices: none -> 15.2 us  [cycle_filter(): jax.lax.all_to_all(jnp.stack([array_here for _ in range(jax.lax.axis_size...]
    squeeze x2 -> x8, local copies, waits for them, and re-layouts: 0.01 us -> 10.8 us  [the longest x2 4.36 us: filter_three(): filtered[1]]
where the time goes in v1:
time: 832 us; the launch traced here: 818 us
  waiting for transfers between devices  548 us (66%)
  local copies, waits for them, and re-layouts  103 us (12%)
  other arithmetic  82.8 us (10%)
  starting transfers between devices  42 us (5%)
  matrix products  40.7 us (5%)
    all_to_all x2, waiting for transfers between devices, cycle_filter(): jax.lax.all_to_all(jnp.stack([array_here for _ in range(jax.lax.axis_size...  548 us
    unnamed x133, local copies, waits for them, and re-layouts  39.8 us
    dot_general x2, matrix products, transform(): jnp.dot(flat, basis, precision=lax.Precision.HIGHEST, preferred_element_t...  36.7 us
    another operation x2, local copies, waits for them, and re-layouts, cycle_filter(): jnp.stack([array_here for _ in range(jax.lax.axis_size(group_axis))])  17.8 us
    another operation x11, local copies, waits for them, and re-layouts, filter_three(): stacked = jnp.stack([first[:, :NF], second[:, :NF], third[:, :NF]])  17 us
    add x1, other arithmetic, local(): keep_factor * electric_azimuth  16.7 us
  transfers between devices with their start and end apart: 10, of which 2 were waited for; matrix products, arithmetic and copies ran while one was open for 11% of the time, Pallas kernels for 0%

profile of v1, /device:TPU:1, one launch (start us, length us, event | category | flops | bytes accessed | tf_op | source)
XLA Modules:
  0.0 818.1 jit_solution(13652951261053159067)
XLA Ops:
  0.7 2.0 copy.74
  2.7 1.5 collective-permute-start
  4.3 1.3 collective-permute-start.1
  7.0 2.0 copy.73
  9.0 6.3 collective-permute-start.3
  15.3 1.3 slice.226
  16.6 1.6 slice.227
  18.2 2.0 copy.77
  20.2 1.4 slice.224
  21.8 3.0 copy.80
  24.8 3.1 copy.86
  27.9 3.1 copy.91
  31.1 6.9 fusion.15
  43.0 1.8 copy.94
  44.8 3.8 slice_bitcast_fusion.4
  48.6 1.8 copy.92
  50.4 1.9 copy.93
  52.4 8.9 %stack.24 = f32[16,3,24,32,128]{4,3,2,1,0:T(8,128)} broadcast(f32[3,24,32,128]{3,2,1,0:T(8,128)S(1)} %pad_maximum_fusion.6), dimensions={1,2,3,4} | broadcast | bytes 20054016 | tf_op jit(solution)/shard_map/stack | solution.py:93
  61.3 6.3 all-to-all-start
  67.7 3.1 copy.65
  72.5 5.3 fusion.40
  77.8 1.6 slice.247
  80.2 1.7 slice.240
  81.8 1.6 slice.234
  83.5 271.1 %all-to-all-done = f32[16,3,24,32,128]{4,3,2,1,0:T(8,128)} async-done(((f32[16,3,24,32,128]{4,3,2,1,0:T(8,128)}), f32[16,3,24,32,128]{4,3,2,1,0:T(8,128)}, u32[]{:S(2)}, u32[]{:S(2)}) %all-to-all-start) | async-done | bytes 18874400 | tf_op jit(solution)/shard_map/all_to_all | solution.py:92
  354.6 18.4 %fusion.6 = f32[3,24,32,256]{3,2,1,0:T(8,128)S(1)} fusion(f32[2048,128]{1,0:T(8,128)S(1)} %get-tuple-element.62, f32[2048,128]{1,0:T(8,128)} %get-tuple-element.63, f32[32,256]{1,0:T(8,128)S(1)} %pad_maximum_fusion.11, f32[16,3,24,32,128]{4,3,2,1,0:T(8,128)} %all-to-all-done), kind=kOutput, calls=%fused_computation.7 | convolution fusion | flops 14496628736 | bytes 23363584 | tf_op jit(solution)/shard_map/dot_general | solution.py:70
  373.0 2.0 fusion.43
  375.1 1.6 copy.100
  376.7 3.7 slice_maximum_fusion.3
  380.7 1.6 slice_maximum_fusion.1
  382.4 1.6 copy.97
  384.0 3.7 slice_maximum_fusion
  388.5 1.6 slice_maximum_fusion.2
  390.1 7.2 collective-permute-start.7
  397.3 4.6 collective-permute-start.6
  402.0 4.1 collective-permute-start.5
  406.1 1.6 copy.96
  407.7 2.5 slice_maximum_fusion.4
  410.2 1.5 fusion.57
  413.0 16.7 %fusion.29 = (f32[24,128,128]{1,0,2:T(8,128)}, f32[24,128,128]{1,0,2:T(8,128)S(1)}, pred[24,128,128]{1,0,2:T(8,128)(4,1)S(1)}, pred[24,128,128]{1,0,2:T(8,128)(4...) fusion(f32[23,128,128]{1,0,2:T(8,128)} %slice_maximum_fusion.1,, ...), kind=kLoop, calls=%fused_computation.42 | loop fusion | flops 16121856 | bytes 17289280 | tf_op jit(solution)/shard_map/add | solution.py:162
  432.3 1.3 copy-done.34
  433.6 13.5 %fusion.33 = f32[24,128,128]{1,0,2:T(8,128)S(1)} fusion(f32[24,128,128]{1,0,2:T(8,128)S(1)} %get-tuple-element.19, f32[24,128,127]{1,0,2:T(8,128)S(1)} %copy-done.34, f32[24,128,1]{1,0,2:T(8,128)} %bitcast.43, f32[24,127,128]{1,0,2:T(8,128)S(1)} %bitcast.95, f32[24,128,128]{1,0,2:T(8,128)S(1)} %copy-done.9, f32[128]{0:T(128)S(1)} %copy-done.55, ...), kind=kLoop, calls=%fused_computation.47 | loop fusion | flops 13369344 | bytes 12572224 | tf_op jit(solution)/shard_map/add | solution.py:165
  449.6 2.6 copy.105
  452.2 16.6 %fusion.26 = (f32[24,128,128]{1,0,2:T(8,128)S(1)}, f32[24,128,128]{1,0,2:T(8,128)}) fusion(f32[24,128,127]{1,0,2:T(8,128)S(1)} %slice_maximum_fusion.4, f32[24,128,1]{1,0,2:T(8,128)S(1)} %bitcast.108, f32[24,128,128]{1,0,2:T(8,128)} %copy-done.10, f32[23,128,128]{1,0,2:T(8,128)} %slice_maximum_fusion.2, f32[1,128,128]{1,0,2:T(1,128)} %bitcast.36, ...), kind=kLoop, calls=%fused_computation.37 | loop fusion | flops 13369344 | bytes 14156352 | tf_op jit(solution)/shard_map/add | solution.py:158
  474.0 8.9 %stack.29 = f32[16,3,24,32,128]{4,3,2,1,0:T(8,128)} broadcast(f32[3,24,32,128]{3,2,1,0:T(8,128)S(1)} %pad_maximum_fusion.7), dimensions={1,2,3,4} | broadcast | bytes 20054016 | tf_op jit(solution)/shard_map/stack | solution.py:93
  482.9 8.9 %all-to-all-start.1 = ((f32[16,3,24,32,128]{4,3,2,1,0:T(8,128)}), f32[16,3,24,32,128]{4,3,2,1,0:T(8,128)}, u32[]{:S(2)}, u32[]{:S(2)}) async-start(f32[16,3,24,32,128]{4,3,2,1,0:T(8,128)} %stack.29), calls=%async_computation.1 | async-start | bytes 37748736 | tf_op jit(solution)/shard_map/all_to_all | solution.py:92
  491.8 1.6 slice.266
  493.5 1.7 slice.264
  495.2 1.6 slice.262
  496.8 1.6 copy.113
  498.4 1.6 copy.114
  500.1 3.2 copy.115
  503.3 276.6 %all-to-all-done.1 = f32[16,3,24,32,128]{4,3,2,1,0:T(8,128)} async-done(((f32[16,3,24,32,128]{4,3,2,1,0:T(8,128)}), f32[16,3,24,32,128]{4,3,2,1,0:T(8,128)}, u32[]{:S(2)}, u32[]{:S(2)}) %all-to-all-start.1) | async-done | bytes 18874400 | tf_op jit(solution)/shard_map/all_to_all | solution.py:92
  779.8 18.3 %fusion.9 = f32[3,24,32,256]{3,2,1,0:T(8,128)S(1)} fusion(f32[2048,128]{1,0:T(8,128)S(1)} %copy-done.28, f32[2048,128]{1,0:T(8,128)S(1)} %copy-done.29, f32[32,256]{1,0:T(8,128)S(1)} %copy-done.44, f32[16,3,24,32,128]{4,3,2,1,0:T(8,128)} %all-to-all-done.1), kind=kOutput, calls=%fused_computation.8 | convolution fusion | flops 14496628736 | bytes 23363584 | tf_op jit(solution)/shard_map/dot_general | solution.py:70
  798.1 2.0 fusion.42
  801.0 1.6 copy.109
  802.6 1.9 pad_maximum_fusion.2
  804.5 1.7 copy.112
  806.1 2.7 copy.108
  808.9 1.9 pad_maximum_fusion.1
  810.8 1.7 copy.111
  812.4 1.6 copy.107
  814.0 1.9 pad_maximum_fusion
  815.9 1.7 copy.110
  (165 shorter events, 22.8 us)
Async XLA Ops:
  0.6 3.5 slice-start.3
  0.6 4.9 slice-start.2
  2.7 15.5 %copy-start.8 = (f32[24,128,128]{1,0,2:T(8,128)}, f32[24,128,128]{1,0,2:T(8,128)S(1)}, u32[]{:S(2)}) copy-start(f32[24,128,128]{1,0,2:T(8,128)S(1)} %copy.74) | copy-start | bytes 4718596
  2.7 28.4 %collective-permute-start = (f32[24,128]{1,0:T(8,128)S(1)}, f32[24,128]{1,0:T(8,128)S(1)}, u32[]{:S(2)}, u32[]{:S(2)}) collective-permute-start(f32[24,128]{1,0:T(8,128)S(1)} %slice_bitcast_fusion.7), channel_id=1, source_target_pairs={{8,0},{16,8},{24,16},{32,24},{40,32},{48,40},{56,48},{64,56},{72,6... | collective-permute-start | bytes 36872 | tf_op jit(solution)/shard_map/ppermute | solution.py:17
  4.3 26.8 %collective-permute-start.1 = (f32[128,128]{0,1:T(8,128)S(1)}, f32[128,128]{0,1:T(8,128)S(1)}, u32[]{:S(2)}, u32[]{:S(2)}) collective-permute-start(f32[128,128]{0,1:T(8,128)S(1)} %bitcast.106), channel_id=1, source_target_pairs={{1,0},{2,1},{3,2},{4,3},{5,4},{6,5},{7,6},{9,8},{10,9},{11,10},{12... | collective-permute-start | bytes 196616 | tf_op jit(solution)/shard_map/ppermute | solution.py:23
  5.7 25.4 %collective-permute-start.2 = (f32[128,128]{0,1:T(8,128)S(1)}, f32[128,128]{0,1:T(8,128)S(1)}, u32[]{:S(2)}, u32[]{:S(2)}) collective-permute-start(f32[128,128]{0,1:T(8,128)S(1)} %bitcast.107), channel_id=1, source_target_pairs={{1,0},{2,1},{3,2},{4,3},{5,4},{6,5},{7,6},{9,8},{10,9},{11,10},{12... | collective-permute-start | bytes 196616 | tf_op jit(solution)/shard_map/ppermute | solution.py:23
  8.9 22.1 %copy-start = (f32[24,128,128]{1,0,2:T(8,128)}, f32[24,128,128]{1,0,2:T(8,128)S(1)}, u32[]{:S(2)}) copy-start(f32[24,128,128]{1,0,2:T(8,128)S(1)} %copy.73) | copy-start | bytes 4718596
  9.0 29.5 %collective-permute-start.3 = (f32[24,128]{1,0:T(8,128)S(1)}, f32[24,128]{1,0:T(8,128)S(1)}, u32[]{:S(2)}, u32[]{:S(2)}) collective-permute-start(f32[24,128]{1,0:T(8,128)S(1)} %slice_bitcast_fusion.6), channel_id=1, source_target_pairs={{8,0},{16,8},{24,16},{32,24},{40,32},{48,40},{56,48},{64,56},{72,6... | collective-permute-start | bytes 36872 | tf_op jit(solution)/shard_map/ppermute | solution.py:17
  15.2 15.8 %copy-start.52 = (f32[128]{0:T(128)}, f32[128]{0:T(128)S(1)}, u32[]{:S(2)}) copy-start(f32[128]{0:T(128)S(1)} %broadcast_multiply_fusion.3) | copy-start | bytes 1540
  15.2 23.2 %copy-start.56 = (f32[128]{0:T(128)}, f32[128]{0:T(128)S(1)}, u32[]{:S(2)}) copy-start(f32[128]{0:T(128)S(1)} %get-tuple-element.61) | copy-start | bytes 1540
  15.3 15.8 %copy-start.54 = (f32[128]{0:T(128)}, f32[128]{0:T(128)S(1)}, u32[]{:S(2)}) copy-start(f32[128]{0:T(128)S(1)} %iota_add_fusion.2) | copy-start | bytes 1540
  20.1 1.7 copy-start.14
  27.9 3.2 slice-start.1
  31.1 7.4 copy-start.30
  38.0 2.0 slice-start
  61.3 293.3 %all-to-all-start = ((f32[16,3,24,32,128]{4,3,2,1,0:T(8,128)}), f32[16,3,24,32,128]{4,3,2,1,0:T(8,128)}, u32[]{:S(2)}, u32[]{:S(2)}) async-start(f32[16,3,24,32,128]{4,3,2,1,0:T(8,128)} %stack.24), calls=%async_computation | async-start | bytes 37748736 | tf_op jit(solution)/shard_map/all_to_all | solution.py:92
  67.6 3.1 copy-start.50
  67.6 3.8 copy-start.51
  67.7 4.4 copy-start.58
  70.7 7.1 copy-start.22
  72.2 282.4 %copy-start.43 = (f32[32,256]{1,0:T(8,128)}, f32[32,256]{1,0:T(8,128)S(1)}, u32[]{:S(2)}) copy-start(f32[32,256]{1,0:T(8,128)S(1)} %pad_maximum_fusion.11) | copy-start | bytes 98308
  72.5 300.5 %copy-start.45 = (f32[128,128]{1,0:T(8,128)}, f32[128,128]{1,0:T(8,128)S(1)}, u32[]{:S(2)}) copy-start(f32[128,128]{1,0:T(8,128)S(1)} %get-tuple-element.56) | copy-start | bytes 196612
  72.5 300.5 %copy-start.47 = (f32[128,128]{1,0:T(8,128)}, f32[128,128]{1,0:T(8,128)S(1)}, u32[]{:S(2)}) copy-start(f32[128,128]{1,0:T(8,128)S(1)} %get-tuple-element.57) | copy-start | bytes 196612
  77.8 276.8 %copy-start.27 = (f32[2048,128]{1,0:T(8,128)}, f32[2048,128]{1,0:T(8,128)S(1)}, u32[]{:S(2)}) copy-start(f32[2048,128]{1,0:T(8,128)S(1)} %get-tuple-element.62) | copy-start | bytes 3145732
  77.8 2.4 copy-start.21
  80.2 1.7 copy-start.18
  376.7 3.7 copy-start.2
  376.7 3.7 copy-start.4
  384.0 3.7 copy-start.6
  384.0 3.7 copy-start.12
  390.1 39.8 %collective-permute-start.7 = (f32[24,128]{1,0:T(8,128)S(1)}, f32[24,128]{1,0:T(8,128)}, u32[]{:S(2)}, u32[]{:S(2)}) collective-permute-start(f32[24,128]{1,0:T(8,128)S(1)} %fusion.58), channel_id=1, source_target_pairs={{120,0},{0,8},{8,16},{16,24},{24,32},{32,40},{40,48},{48,56},{56,6... | collective-permute-start | bytes 36872 | tf_op jit(solution)/shard_map/ppermute | solution.py:17
  397.3 15.0 %collective-permute-start.6 = (f32[128,128]{0,1:T(8,128)S(1)}, f32[128,128]{0,1:T(8,128)S(1)}, u32[]{:S(2)}, u32[]{:S(2)}) collective-permute-start(f32[128,128]{0,1:T(8,128)S(1)} %bitcast.105), channel_id=1, source_target_pairs={{0,1},{1,2},{2,3},{3,4},{4,5},{5,6},{6,7},{8,9},{9,10},{10,11},{11... | collective-permute-start | bytes 196616 | tf_op jit(solution)/shard_map/ppermute | solution.py:23
  402.0 50.2 %collective-permute-start.5 = (f32[128,128]{0,1:T(8,128)}, f32[128,128]{0,1:T(8,128)}, u32[]{:S(2)}, u32[]{:S(2)}) collective-permute-start(f32[128,128]{0,1:T(8,128)} %bitcast.35), channel_id=1, source_target_pairs={{0,1},{1,2},{2,3},{3,4},{4,5},{5,6},{6,7},{8,9},{9,10},{10,11},{11... | collective-permute-start | bytes 196616 | tf_op jit(solution)/shard_map/ppermute | solution.py:23
  407.7 5.3 copy-start.7
  407.7 5.3 copy-start.13
  407.7 5.3 copy-start.15
  410.2 2.8 copy-start.3
  410.2 2.8 copy-start.5
  411.8 40.4 %collective-permute-start.4 = (f32[24,128]{1,0:T(8,128)}, f32[24,128]{1,0:T(8,128)S(1)}, u32[]{:S(2)}, u32[]{:S(2)}) collective-permute-start(f32[24,128]{1,0:T(8,128)} %fusion.57), channel_id=1, source_target_pairs={{120,0},{0,8},{8,16},{16,24},{24,32},{32,40},{40,48},{48,56},{56,6... | collective-permute-start | bytes 36872 | tf_op jit(solution)/shard_map/ppermute | solution.py:17
  429.7 1.7 copy-start.23
  429.7 17.5 %copy-start.35 = (pred[24,128,128]{1,0,2:T(8,128)(4,1)}, pred[24,128,128]{1,0,2:T(8,128)(4,1)S(1)}, u32[]{:S(2)}) copy-start(pred[24,128,128]{1,0,2:T(8,128)(4,1)S(1)} %get-tuple-element.21) | copy-start | bytes 1179652
  429.7 17.5 %copy-start.36 = (pred[24,128,128]{1,0,2:T(8,128)(4,1)}, pred[24,128,128]{1,0,2:T(8,128)(4,1)S(1)}, u32[]{:S(2)}) copy-start(pred[24,128,128]{1,0,2:T(8,128)(4,1)S(1)} %get-tuple-element.22) | copy-start | bytes 1179652
  429.7 17.5 %copy-start.37 = (pred[24,128,128]{1,0,2:T(8,128)(4,1)}, pred[24,128,128]{1,0,2:T(8,128)(4,1)S(1)}, u32[]{:S(2)}) copy-start(pred[24,128,128]{1,0,2:T(8,128)(4,1)S(1)} %get-tuple-element.23) | copy-start | bytes 1179652
  429.7 17.5 %copy-start.38 = (pred[24,128,128]{1,0,2:T(8,128)(4,1)}, pred[24,128,128]{1,0,2:T(8,128)(4,1)S(1)}, u32[]{:S(2)}) copy-start(pred[24,128,128]{1,0,2:T(8,128)(4,1)S(1)} %get-tuple-element.24) | copy-start | bytes 1179652
  429.7 17.5 %copy-start.39 = (pred[24,128,128]{1,0,2:T(8,128)(4,1)}, pred[24,128,128]{1,0,2:T(8,128)(4,1)S(1)}, u32[]{:S(2)}) copy-start(pred[24,128,128]{1,0,2:T(8,128)(4,1)S(1)} %get-tuple-element.25) | copy-start | bytes 1179652
  429.7 17.5 %copy-start.40 = (pred[24,128,128]{1,0,2:T(8,128)(4,1)}, pred[24,128,128]{1,0,2:T(8,128)(4,1)S(1)}, u32[]{:S(2)}) copy-start(pred[24,128,128]{1,0,2:T(8,128)(4,1)S(1)} %get-tuple-element.26) | copy-start | bytes 1179652
  429.7 17.5 %copy-start.41 = (pred[24,128,128]{1,0,2:T(8,128)(4,1)}, pred[24,128,128]{1,0,2:T(8,128)(4,1)S(1)}, u32[]{:S(2)}) copy-start(pred[24,128,128]{1,0,2:T(8,128)(4,1)S(1)} %get-tuple-element.27) | copy-start | bytes 1179652
  429.7 2.6 copy-start.9
  429.7 3.9 copy-start.34
  429.7 3.9 copy-start.53
  429.8 3.9 copy-start.55
  449.6 2.6 copy-start.57
  482.9 8.9 %copy-start.26 = (f32[24,128,128]{1,0,2:T(8,128)S(1)}, f32[24,128,128]{1,0,2:T(8,128)}, u32[]{:S(2)}) copy-start(f32[24,128,128]{1,0,2:T(8,128)} %copy-done.25) | copy-start | bytes 4718596
  482.9 296.9 %all-to-all-start.1 = ((f32[16,3,24,32,128]{4,3,2,1,0:T(8,128)}), f32[16,3,24,32,128]{4,3,2,1,0:T(8,128)}, u32[]{:S(2)}, u32[]{:S(2)}) async-start(f32[16,3,24,32,128]{4,3,2,1,0:T(8,128)} %stack.29), calls=%async_computation.1 | async-start | bytes 37748736 | tf_op jit(solution)/shard_map/all_to_all | solution.py:92
  493.5 1.7 copy-start.20
  495.2 1.6 copy-start.24
  496.8 1.7 copy-start.11
  500.1 279.7 %copy-start.28 = (f32[2048,128]{1,0:T(8,128)S(1)}, f32[2048,128]{1,0:T(8,128)}, u32[]{:S(2)}) copy-start(f32[2048,128]{1,0:T(8,128)} %copy-done.27) | copy-start | bytes 3145732
  500.1 279.7 %copy-start.29 = (f32[2048,128]{1,0:T(8,128)S(1)}, f32[2048,128]{1,0:T(8,128)}, u32[]{:S(2)}) copy-start(f32[2048,128]{1,0:T(8,128)} %get-tuple-element.63) | copy-start | bytes 3145732
  500.1 279.7 %copy-start.44 = (f32[32,256]{1,0:T(8,128)S(1)}, f32[32,256]{1,0:T(8,128)}, u32[]{:S(2)}) copy-start(f32[32,256]{1,0:T(8,128)} %copy-done.43) | copy-start | bytes 98308
  503.3 294.9 %copy-start.46 = (f32[128,128]{1,0:T(8,128)S(1)}, f32[128,128]{1,0:T(8,128)}, u32[]{:S(2)}) copy-start(f32[128,128]{1,0:T(8,128)} %copy-done.45) | copy-start | bytes 196612
  503.3 294.9 %copy-start.48 = (f32[128,128]{1,0:T(8,128)S(1)}, f32[128,128]{1,0:T(8,128)}, u32[]{:S(2)}) copy-start(f32[128,128]{1,0:T(8,128)} %copy-done.47) | copy-start | bytes 196612
  801.0 1.6 copy-start.33
  806.1 2.7 copy-start.32
  (9 other events, 10.9 us)
